TPU v7x, 256 devices: a whole 4x4x8 slice. The times are simulated.
256 devices in a mesh: ctx: 32 (over x, z), head: 8 (over y, core).
Axes of the slice: x: 4, y: 4, z: 8, core: 2. Of those that a mesh axis runs over, the one named last changes fastest.
Arguments:
- queries: float32 [32768, 768], P(('ctx', 'head')), may hold values from -280 to 280, as said below
- keys: float32 [32768, 768], P(('ctx', 'head')), may hold values from -7 to 7, as said below
- values: float32 [32768, 768], P(('ctx', 'head')), may hold values from -6 to 6
- grad_out: float32 [32768, 768], P(('ctx', 'head')), may hold values from -6 to 6
- neighbours: int32 [256, 2], replicated, may hold values from 0 to 255, as said below
- bias_index: int32 [256, 3], P('ctx'), may hold values from 0 to 15
- bias_table: float32 [16, 128, 128], replicated, may hold values from -6 to 6
- head_gain: float32 [16], P('head'), may hold values from 0.5 to 2
Outputs:
- attended: float32 [32768, 768], P(('ctx', 'head'))
- grad_queries: float32 [32768, 768], P(('ctx', 'head'))
- grad_keys: float32 [32768, 768], P(('ctx', 'head'))
- grad_values: float32 [32768, 768], P(('ctx', 'head'))
- grad_table: float32 [16, 128, 128], replicated
- grad_gain: float32 [16], P('head')
Inputs may be any that keep to these rules, and one draw needn't show every extreme that they name: `neighbours`: each entry names a block of another ctx shard (entry // 8 differs from the query block's b // 8). Among the rows of one ctx shard, at most 1 entries name blocks of one other shard, and at most 1 distinct blocks of it; both bounds are reached in every draw. `queries`: entries have magnitude at most 280. `keys`: entries have magnitude at most 7.
All inputs are finite; a program needn't handle non-finite values.
Results may differ from a plain program's by a relative error of at most 0.0003.
Values sent between devices are 32-bit elements; how exact they have to be, the bound alone decides.
A program may use at most 128 MiB of HBM per device.

v0:
```python
from functools import partial
import jax
import jax.numpy as jnp
from jax import lax
from jax.sharding import PartitionSpec as P

BLOCK = 128
NEI = 2


def attend(query_block, key_sets, value_sets, edge_bias, head_gain):
    head_count = head_gain.shape[0]
    block_rows = query_block.shape[0]
    set_blocks = key_sets.shape[0]
    query_heads = query_block.reshape(block_rows, head_count, -1)
    key_heads = key_sets.reshape(set_blocks, block_rows, head_count, -1)
    value_heads = value_sets.reshape(set_blocks * block_rows, head_count, -1)
    factor = query_heads.shape[2] ** (-0.5)
    scores = (
        jnp.einsum("ihd,mchd->himc", query_heads, key_heads, precision=lax.Precision.HIGHEST)
        * factor
    )
    scores = scores + head_gain[:, None, None, None] * jnp.transpose(edge_bias, (1, 0, 2))[None]
    scores = scores.reshape(head_count, block_rows, set_blocks * block_rows)
    maxima = lax.stop_gradient(jnp.max(scores, axis=-1, keepdims=True))
    weights = jnp.exp(scores - maxima)
    weights = weights / jnp.sum(weights, axis=-1, keepdims=True)
    result = jnp.einsum("hik,khd->ihd", weights, value_heads, precision=lax.Precision.HIGHEST)
    return result.reshape(block_rows, -1)


def request_slots(requests, blocks):
    owners = requests // blocks
    ordinal = jnp.arange(requests.shape[0], dtype=jnp.int32)
    earlier = ordinal[None, :] < ordinal[:, None]
    same_owner = owners[:, None] == owners[None, :]
    return jnp.sum((same_owner & earlier).astype(jnp.int32), axis=1)


def body(queries, keys, values, grad_out, neighbours, bias_index, bias_table, head_gain):
    shards = lax.axis_size("ctx")
    myself = lax.axis_index("ctx")
    head_query, head_key, head_value, head_grad = (
        lax.all_to_all(queries, "head", split_axis=1, concat_axis=0, tiled=True),
        lax.all_to_all(keys, "head", split_axis=1, concat_axis=0, tiled=True),
        lax.all_to_all(values, "head", split_axis=1, concat_axis=0, tiled=True),
        lax.all_to_all(grad_out, "head", split_axis=1, concat_axis=0, tiled=True),
    )
    length, columns = head_query.shape
    blocks = length // BLOCK
    requests = blocks * NEI
    capacity = (requests + shards - 2) // (shards - 1)
    all_requests = neighbours.reshape(shards, requests)
    slot_all = jax.vmap(partial(request_slots, blocks=blocks))(all_requests)
    owners = all_requests // blocks
    local_ids = all_requests % blocks
    from_me = owners == myself
    slot_ids = jnp.arange(capacity, dtype=jnp.int32)
    selected = from_me[:, None, :] & (slot_all[:, None, :] == slot_ids[None, :, None])
    send_ids = jnp.max(jnp.where(selected, local_ids[:, None, :], 0), axis=2).reshape(-1)
    filled = jnp.any(selected, axis=2).reshape(-1)
    packed = jnp.concatenate([head_key, head_value], axis=1).reshape(blocks, BLOCK, 2 * columns)
    outgoing = jnp.where(filled[:, None, None], packed[send_ids], 0.0)
    arrived = lax.all_to_all(outgoing, "ctx", split_axis=0, concat_axis=0, tiled=True)
    my_owners = lax.dynamic_index_in_dim(owners, myself, 0, keepdims=False)
    my_slots = lax.dynamic_index_in_dim(slot_all, myself, 0, keepdims=False)
    wanted = my_owners * capacity + my_slots
    remote = arrived[wanted].reshape(blocks, NEI, BLOCK, 2 * columns)
    gathered = jnp.concatenate([packed[:, None], remote], axis=1)
    edge_bias = bias_table[bias_index]
    forward = jax.vmap(attend, in_axes=(0, 0, 0, 0, None))
    result, pullback = jax.vjp(
        forward,
        head_query.reshape(blocks, BLOCK, columns),
        gathered[..., :columns],
        gathered[..., columns:],
        edge_bias,
        head_gain,
    )
    query_grad, key_grad, value_grad, bias_grad, gain_grad = pullback(
        head_grad.reshape(blocks, BLOCK, columns)
    )
    attended, grad_queries = (
        lax.all_to_all(
            result.reshape(length, columns), "head", split_axis=0, concat_axis=1, tiled=True
        ),
        lax.all_to_all(
            query_grad.reshape(length, columns), "head", split_axis=0, concat_axis=1, tiled=True
        ),
    )
    remote_grad = jnp.concatenate([key_grad[:, 1:], value_grad[:, 1:]], axis=3).reshape(
        requests, BLOCK, 2 * columns
    )
    returning = (
        jnp.zeros((shards * capacity, BLOCK, 2 * columns), jnp.float32).at[wanted].add(remote_grad)
    )
    returned = lax.all_to_all(returning, "ctx", split_axis=0, concat_axis=0, tiled=True)
    local_grad = jnp.concatenate([key_grad[:, 0], value_grad[:, 0]], axis=2)
    local_grad = local_grad.at[send_ids].add(jnp.where(filled[:, None, None], returned, 0.0))
    local_grad = local_grad.reshape(length, 2 * columns)
    grad_keys, grad_values = (
        lax.all_to_all(local_grad[:, :columns], "head", split_axis=0, concat_axis=1, tiled=True),
        lax.all_to_all(local_grad[:, columns:], "head", split_axis=0, concat_axis=1, tiled=True),
    )
    table_grad = (
        jnp.zeros(bias_table.shape, jnp.float32)
        .at[bias_index.reshape(-1)]
        .add(bias_grad.reshape(-1, BLOCK, BLOCK))
    )
    grad_table = lax.psum(table_grad, ("ctx", "head"))
    grad_gain = lax.psum(gain_grad, "ctx")
    return (attended, grad_queries, grad_keys, grad_values, grad_table, grad_gain)


def solution(mesh):
    return jax.shard_map(
        body,
        mesh=mesh,
        in_specs=(
            P(("ctx", "head"), None),
            P(("ctx", "head"), None),
            P(("ctx", "head"), None),
            P(("ctx", "head"), None),
            P(),
            P("ctx", None),
            P(),
            P("head"),
        ),
        out_specs=(
            P(("ctx", "head"), None),
            P(("ctx", "head"), None),
            P(("ctx", "head"), None),
            P(("ctx", "head"), None),
            P(),
            P("head"),
        ),
        check_vma=False,
    )
```

profile of v0, /device:TPU:2, one launch (start us, length us, event | category | flops | bytes accessed | tf_op | source)
XLA Modules:
  0.0 574.3 jit_solution(18262318619627758660)
XLA Ops:
  7.2 2.0 copy.154
  9.2 4.5 all-to-all-start.1
  14.8 1.9 copy.153
  16.9 5.6 all-to-all-done.1
  22.6 3.5 all-to-all-start
  26.1 8.8 %all-to-all-done = f32[128,8,96]{0,2,1:T(8,128)S(1)} async-done(((f32[128,8,96]{0,2,1:T(8,128)}), f32[128,8,96]{0,2,1:T(8,128)S(1)}, u32[]{:S(2)}, u32[]{:S(2)}) %all-to-all-start) | async-done | bytes 393248 | tf_op jit(solution)/shard_map/all_to_all | solution.py:45
  34.9 2.4 gather_fusion
  37.4 4.0 broadcast_select_fusion.1
  41.4 11.8 %all-to-all-start.2 = ((f32[32,128,192]{1,2,0:T(8,128)}), f32[32,128,192]{1,2,0:T(8,128)}, u32[]{:S(2)}, u32[]{:S(2)}) async-start(f32[32,128,192]{1,2,0:T(8,128)} %broadcast_select_fusion.1), calls=%async_computation.2 | async-start | bytes 6291456 | tf_op jit(solution)/shard_map/all_to_all | solution.py:64
  53.4 0.9 copy.167
  54.5 70.2 %all-to-all-done.2 = f32[32,128,192]{1,2,0:T(8,128)} async-done(((f32[32,128,192]{1,2,0:T(8,128)}), f32[32,128,192]{1,2,0:T(8,128)}, u32[]{:S(2)}, u32[]{:S(2)}) %all-to-all-start.2) | async-done | bytes 3145760 | tf_op jit(solution)/shard_map/all_to_all | solution.py:64
  124.7 3.5 all-to-all-start.3
  128.9 1.6 copy.170
  131.5 2.5 gather_fusion.1
  134.1 1.6 pad_maximum_fusion.2
  135.7 1.4 all-to-all-done.3
  137.0 3.5 all-to-all-start.5
  140.5 7.1 %fusion.19 = (f32[8,2,128]{2,1,0:T(2,128)S(1)}, f32[8,2,128,3,128]{2,4,3,1,0:T(8,128)S(1)}) fusion(f32[8,128,3,128]{1,3,2,0:T(8,128)} %bitcast.132, f32[2]{0:T(128)S(1)} %copy-done.21, f32[8,128,2,48,1]{1,3,4,2,0:T(8,128)} %bitcast.145, f32[8,3,128,2,48]{2,4,3,1,0:T(8,128)} %bitcast.134), kind=kOutput, calls=%fused_computation.74 | convolution fusion | flops 456128512 | bytes 6299656 | tf_op jit(solution)/shard_map/jvp(vmap(ihd,mchd->himc))/dot_general | solution.py:20
  148.8 2.0 copy.166
  150.8 3.1 reshape.372
  154.6 6.8 %fusion = (f32[8,2,128]{2,1,0:T(2,128)S(1)}, f32[8,2,384,128]{3,2,1,0:T(8,128)S(1)}) fusion(f32[8,2,128,3,128]{2,4,3,1,0:T(8,128)S(1)} %get-tuple-element.50, f32[8,2,128]{2,1,0:T(2,128)} %multiply_divide_fusion, f32[8,2,128]{2,1,0:T(2,128)S(1)} %get-tuple-element.49, f32[8,384,2,48]{1,3,2,0:T(8,128)} %reshape.372, f32[8,2,48,128]{3,2,1,0:T(8,128)S(1)} %bitcast.143), kind=kOutput, calls=%fused_computation.8 | convolution fusion | flops 456128512 | bytes 7888896 | tf_op jit(solution)/shard_map/transpose(jvp(vmap(hik,khd->ihd)))/dot_general | solution.py:28
  161.5 2.9 multiply_reduce_fusion
  164.7 1.3 copy-done.4
  166.0 5.0 convolution_bitcast_fusion
  171.0 3.3 reshape.376
  174.3 5.1 convolution_bitcast_fusion.1
  180.2 2.0 broadcast_in_dim.27
  182.2 4.1 scatter_fusion
  186.3 8.0 %all-to-all-start.7 = ((f32[32,128,192]{1,2,0:T(8,128)}), f32[32,128,192]{1,2,0:T(8,128)}, u32[]{:S(2)}, u32[]{:S(2)}) async-start(f32[32,128,192]{1,2,0:T(8,128)} %scatter_fusion), calls=%async_computation.7 | async-start | bytes 6291456 | tf_op jit(solution)/shard_map/all_to_all | solution.py:97
  194.7 1.0 copy-done.8
  195.6 5.2 fusion.20
  200.9 3.0 fusion.4
  203.9 63.0 %all-to-all-done.7 = f32[32,128,192]{1,2,0:T(8,128)} async-done(((f32[32,128,192]{1,2,0:T(8,128)}), f32[32,128,192]{1,2,0:T(8,128)}, u32[]{:S(2)}, u32[]{:S(2)}) %all-to-all-start.7) | async-done | bytes 3145760 | tf_op jit(solution)/shard_map/all_to_all | solution.py:97
  266.9 4.4 all-to-all-start.4
  271.4 4.0 broadcast_select_fusion
  275.4 5.6 scatter_fusion.1
  281.0 5.1 all-to-all-start.6
  287.8 7.2 %all-to-all-done.6 = f32[8,128,96]{1,2,0:T(8,128)S(1)} async-done(((f32[8,128,96]{1,2,0:T(8,128)}), f32[8,128,96]{1,2,0:T(8,128)S(1)}, u32[]{:S(2)}, u32[]{:S(2)}) %all-to-all-start.6) | async-done | bytes 393248 | tf_op jit(solution)/shard_map/all_to_all | solution.py:87
  295.0 3.5 all-to-all-start.8
  298.8 1.6 copy.185
  300.6 4.5 scatter_fusion.2
  305.1 1.0 copy-done.6
  306.1 1.9 copy.211
  308.0 4.7 all-to-all-start.9
  312.6 62.4 %psum.15 = f32[2]{0:T(128)} all-reduce(f32[2]{0:T(128)S(1)} %copy-done.27), channel_id=1, replica_groups=mesh['ctx'=32,'head'=8] {'ctx'}, use_global_device_ids=true, to_apply=%region_12.13 | all-reduce | flops 2 | bytes 16 | tf_op jit(solution)/shard_map/psum | solution.py:111
  377.7 0.9 copy.189
  378.7 186.3 %all-reduce.2.cloned.1.call-done = f32[16,128,128]{2,1,0:T(8,128)} async-done(((f32[16,128,128]{2,1,0:T(8,128)}), f32[16,128,128]{2,1,0:T(8,128)}) %all-reduce.2.cloned.1.call-update) | async-done | bytes 1048592 | tf_op jit(solution)/shard_map/psum | solution.py:110
  565.0 2.3 copy.217
  (107 shorter events, 11.6 us)
Async XLA Ops:
  7.2 121.0 %copy-start = (f32[16,128,128]{2,1,0:T(8,128)S(1)}, f32[16,128,128]{2,1,0:T(8,128)}, u32[]{:S(2)}) copy-start(f32[16,128,128]{2,1,0:T(8,128)} %param.14) | copy-start | bytes 3145732
  9.2 13.4 %all-to-all-start.1 = ((f32[128,8,96]{0,2,1:T(8,128)}), f32[128,8,96]{0,2,1:T(8,128)S(1)}, u32[]{:S(2)}, u32[]{:S(2)}) async-start(f32[128,8,96]{0,2,1:T(8,128)} %bitcast.3), calls=%async_computation.1 | async-start | bytes 786432 | tf_op jit(solution)/shard_map/all_to_all | solution.py:46
  16.9 20.4 %copy-start.19 = (pred[32]{0:T(512)(128)(4,1)}, pred[32]{0:T(512)(128)(4,1)S(1)}, u32[]{:S(2)}) copy-start(pred[32]{0:T(512)(128)(4,1)S(1)} %get-tuple-element.39) | copy-start | bytes 100
  22.6 12.3 %all-to-all-start = ((f32[128,8,96]{0,2,1:T(8,128)}), f32[128,8,96]{0,2,1:T(8,128)S(1)}, u32[]{:S(2)}, u32[]{:S(2)}) async-start(f32[128,8,96]{0,2,1:T(8,128)} %bitcast), calls=%async_computation | async-start | bytes 786432 | tf_op jit(solution)/shard_map/all_to_all | solution.py:45
  26.1 11.3 %copy-start.23 = (s32[32]{0:T(128)}, s32[32]{0:T(128)S(1)}, u32[]{:S(2)}) copy-start(s32[32]{0:T(128)S(1)} %fusion.14) | copy-start | bytes 388
  34.9 2.5 copy-start.13
  41.4 11.8 %copy-start.17 = (s32[8,3]{0,1:T(4,128)S(1)}, s32[8,3]{0,1:T(4,128)}, u32[]{:S(2)}) copy-start(s32[8,3]{0,1:T(4,128)} %param.13) | copy-start | bytes 292
  41.4 12.0 %copy-start.15 = (f32[128,768]{1,0:T(8,128)S(1)}, f32[128,768]{1,0:T(8,128)}, u32[]{:S(2)}) copy-start(f32[128,768]{1,0:T(8,128)} %param.8) | copy-start | bytes 1179652
  41.4 83.4 %all-to-all-start.2 = ((f32[32,128,192]{1,2,0:T(8,128)}), f32[32,128,192]{1,2,0:T(8,128)}, u32[]{:S(2)}, u32[]{:S(2)}) async-start(f32[32,128,192]{1,2,0:T(8,128)} %broadcast_select_fusion.1), calls=%async_computation.2 | async-start | bytes 6291456 | tf_op jit(solution)/shard_map/all_to_all | solution.py:64
  54.5 70.3 %copy-start.25 = (s32[16]{0:T(128)}, s32[16]{0:T(128)S(1)}, u32[]{:S(2)}) copy-start(s32[16]{0:T(128)S(1)} %fusion.15) | copy-start | bytes 196
  124.7 12.3 %all-to-all-start.3 = ((f32[128,8,96]{0,2,1:T(8,128)}), f32[128,8,96]{0,2,1:T(8,128)S(1)}, u32[]{:S(2)}, u32[]{:S(2)}) async-start(f32[128,8,96]{0,2,1:T(8,128)} %bitcast.13), calls=%async_computation.3 | async-start | bytes 786432 | tf_op jit(solution)/shard_map/all_to_all | solution.py:44
  128.9 1.7 copy-start.16
  128.9 2.6 copy-start.14
  134.0 6.5 %copy-start.21 = (f32[2]{0:T(128)S(1)}, f32[2]{0:T(128)}, u32[]{:S(2)}) copy-start(f32[2]{0:T(128)} %param.15) | copy-start | bytes 28
  137.0 3.5 copy-start.12
  137.0 17.6 %all-to-all-start.5 = ((f32[128,8,96]{0,2,1:T(8,128)}), f32[128,8,96]{0,2,1:T(8,128)S(1)}, u32[]{:S(2)}, u32[]{:S(2)}) async-start(f32[128,8,96]{0,2,1:T(8,128)} %bitcast.154), calls=%async_computation.5 | async-start | bytes 786432 | tf_op jit(solution)/shard_map/all_to_all | solution.py:47
  147.6 1.3 copy-start.11
  154.6 6.8 %copy-start.5 = (f32[8,3,128,128]{2,3,1,0:T(8,128)S(1)}, f32[8,3,128,128]{2,3,1,0:T(8,128)}, u32[]{:S(2)}) copy-start(f32[8,3,128,128]{2,3,1,0:T(8,128)} %copy.170) | copy-start | bytes 4718596
  154.6 6.9 %copy-start.22 = (f32[2]{0:T(128)S(1)}, f32[2]{0:T(128)}, u32[]{:S(2)}) copy-start(f32[2]{0:T(128)} %param.15) | copy-start | bytes 28
  164.4 1.6 copy-start.4
  164.7 9.5 %copy-start.2 = (f32[8,2,128,384]{2,3,1,0:T(8,128)}, f32[8,2,128,384]{2,3,1,0:T(8,128)S(1)}, u32[]{:S(2)}) copy-start(f32[8,2,128,384]{2,3,1,0:T(8,128)S(1)} %broadcast_multiply_fusion) | copy-start | bytes 9437188
  174.3 5.2 copy-start.10
  180.1 2.2 copy-start.26
  186.3 8.1 %copy-start.18 = (s32[8,3]{0,1:T(4,128)S(1)}, s32[8,3]{0,1:T(4,128)}, u32[]{:S(2)}) copy-start(s32[8,3]{0,1:T(4,128)} %param.13) | copy-start | bytes 292
  186.3 8.3 %slice-start = ((f32[8,3,128,96]{2,1,3,0:T(4,128)}), f32[8,1,128,96]{2,1,3,0:T(1,128)S(1)}, s32[]{:S(2)}) async-start(f32[8,3,128,96]{2,1,3,0:T(4,128)} %reshape.376), calls=%async_computation.11 | async-start | bytes 786432 | tf_op jit(solution)/shard_map/slice | solution.py:98
  186.3 80.6 %all-to-all-start.7 = ((f32[32,128,192]{1,2,0:T(8,128)}), f32[32,128,192]{1,2,0:T(8,128)}, u32[]{:S(2)}, u32[]{:S(2)}) async-start(f32[32,128,192]{1,2,0:T(8,128)} %scatter_fusion), calls=%async_computation.7 | async-start | bytes 6291456 | tf_op jit(solution)/shard_map/all_to_all | solution.py:97
  194.4 1.3 copy-start.8
  194.6 6.3 %copy-start.3 = (f32[8,2,128,384]{2,3,1,0:T(8,128)S(1)}, f32[8,2,128,384]{2,3,1,0:T(8,128)}, u32[]{:S(2)}) copy-start(f32[8,2,128,384]{2,3,1,0:T(8,128)} %copy-done.2) | copy-start | bytes 9437188
  194.6 6.3 %copy-start.7 = (f32[8,3,128,96]{2,3,1,0:T(8,128)S(1)}, f32[8,3,128,96]{2,3,1,0:T(8,128)}, u32[]{:S(2)}) copy-start(f32[8,3,128,96]{2,3,1,0:T(8,128)} %get-tuple-element.42) | copy-start | bytes 3538948
  200.9 70.5 %copy-start.20 = (pred[32]{0:T(512)(128)(4,1)S(1)}, pred[32]{0:T(512)(128)(4,1)}, u32[]{:S(2)}) copy-start(pred[32]{0:T(512)(128)(4,1)} %copy-done.19) | copy-start | bytes 100
  266.9 14.0 %all-to-all-start.4 = ((f32[8,128,96]{1,2,0:T(8,128)}), f32[8,128,96]{1,2,0:T(8,128)S(1)}, u32[]{:S(2)}, u32[]{:S(2)}) async-start(f32[8,128,96]{1,2,0:T(8,128)} %bitcast.23), calls=%async_computation.4 | async-start | bytes 786432 | tf_op jit(solution)/shard_map/all_to_all | solution.py:84
  271.4 4.0 copy-start.24
  281.0 17.6 %copy-start.9 = (f32[8,128,384]{1,2,0:T(8,128)S(1)}, f32[8,128,384]{1,2,0:T(8,128)}, u32[]{:S(2)}) copy-start(f32[8,128,384]{1,2,0:T(8,128)} %get-tuple-element.37) | copy-start | bytes 4718596
  281.0 14.0 %all-to-all-start.6 = ((f32[8,128,96]{1,2,0:T(8,128)}), f32[8,128,96]{1,2,0:T(8,128)S(1)}, u32[]{:S(2)}, u32[]{:S(2)}) async-start(f32[8,128,96]{1,2,0:T(8,128)} %bitcast.36), calls=%async_computation.6 | async-start | bytes 786432 | tf_op jit(solution)/shard_map/all_to_all | solution.py:87
  295.0 12.9 %all-to-all-start.8 = ((f32[8,128,96]{1,2,0:T(8,128)}), f32[8,128,96]{1,2,0:T(8,128)S(1)}, u32[]{:S(2)}, u32[]{:S(2)}) async-start(f32[8,128,96]{1,2,0:T(8,128)} %bitcast.129), calls=%async_computation.8 | async-start | bytes 786432 | tf_op jit(solution)/shard_map/all_to_all | solution.py:102
  298.5 266.5 %all-reduce.2.cloned.1.call-start = ((), (), s32[]{:S(2)}) async-start(), calls=%async_computation.10 | async-start | bytes 2097152 | tf_op jit(solution)/shard_map/psum | solution.py:110
  300.5 12.1 %copy-start.27 = (f32[2]{0:T(128)S(1)}, f32[2]{0:T(128)}, u32[]{:S(2)}) copy-start(f32[2]{0:T(128)} %get-tuple-element.36) | copy-start | bytes 28
  305.0 1.0 copy-start.6
  306.0 261.2 %copy-start.1 = (f32[16,128,128]{2,1,0:T(8,128)S(1)}, f32[16,128,128]{2,1,0:T(8,128)}, u32[]{:S(2)}) copy-start(f32[16,128,128]{2,1,0:T(8,128)} %param.14) | copy-start | bytes 3145732
  308.0 69.8 %all-to-all-start.9 = ((f32[8,128,96]{1,2,0:T(8,128)}), f32[8,128,96]{1,2,0:T(8,128)S(1)}, u32[]{:S(2)}, u32[]{:S(2)}) async-start(f32[8,128,96]{1,2,0:T(8,128)} %bitcast.128), calls=%async_computation.9 | async-start | bytes 786432 | tf_op jit(solution)/shard_map/all_to_all | solution.py:103
Sparse Core Ops, SparseCore 0:
  306.2 258.7 all-reduce.1
where the time goes:
time: 583 us; the launch traced here: 574 us
  waiting for transfers between devices  343 us (59%)
  blocking collectives  62.4 us (11%)
  starting transfers between devices  52.4 us (9%)
  local copies, waits for them, and re-layouts  41.1 us (7%)
  matrix products  32.2 us (6%)
  other arithmetic  28.8 us (5%)
  between operations  14.8 us (3%)
    psum x1, waiting for transfers between devices, body(): grad_table = lax.psum(table_grad, ('ctx', 'head'))  186 us
    all_to_all x1, waiting for transfers between devices, body(): lax.all_to_all(outgoing, 'ctx', split_axis=0, concat_axis=0, tiled=True)  70.2 us
    all_to_all x1, waiting for transfers between devices, body(): lax.all_to_all(returning, 'ctx', split_axis=0, concat_axis=0, tiled=True)  63 us
    psum x1, blocking collectives, body(): grad_gain = lax.psum(gain_grad, 'ctx')  62.4 us
    unnamed x69, local copies, waits for them, and re-layouts  17.6 us
    dot_general x3, matrix products, attend(): jnp.einsum('hik,khd->ihd', weights, value_heads, precision=lax.Precision....  17 us
    dot_general x3, matrix products, attend(): jnp.einsum('ihd,mchd->himc', query_heads, key_heads, precision=lax.Precis...  15.2 us
    all_to_all x1, starting transfers between devices, body(): lax.all_to_all(outgoing, 'ctx', split_axis=0, concat_axis=0, tiled=True)  11.8 us
  transfers between devices with their start and end apart: 11, of which 7 were waited for; matrix products, arithmetic and copies ran while one was open for 10% of the time, Pallas kernels for 0%

commit v1 on v0

--- a/solution.py
+++ b/solution.py
@@ -107,7 +107,7 @@
         .at[bias_index.reshape(-1)]
         .add(bias_grad.reshape(-1, BLOCK, BLOCK))
     )
-    grad_table = lax.psum(table_grad, ("ctx", "head"))
+    grad_table = lax.psum(lax.psum(table_grad, "ctx"), "head")
     grad_gain = lax.psum(gain_grad, "ctx")
     return (attended, grad_queries, grad_keys, grad_values, grad_table, grad_gain)
 

time: 583 us -> 467 us (0.80)
  the two profiles are of different devices: /device:TPU:2 before, /device:TPU:8 now
where the time goes in v1:
time: 467 us; the launch traced here: 458 us
  waiting for transfers between devices  214 us (46%)
  blocking collectives  72.7 us (16%)
  starting transfers between devices  56.1 us (12%)
  local copies, waits for them, and re-layouts  39.5 us (8%)
  matrix products  32 us (7%)
  other arithmetic  28.8 us (6%)
  between operations  14.8 us (3%)
    all_to_all x1, waiting for transfers between devices, body(): lax.all_to_all(outgoing, 'ctx', split_axis=0, concat_axis=0, tiled=True)  72.7 us
    psum x1, blocking collectives, body(): grad_gain = lax.psum(gain_grad, 'ctx')  72.7 us
    all_to_all x1, waiting for transfers between devices, body(): lax.all_to_all(returning, 'ctx', split_axis=0, concat_axis=0, tiled=True)  64.7 us
    psum x2, waiting for transfers between devices, body(): grad_table = lax.psum(lax.psum(table_grad, 'ctx'), 'head')  58.3 us
    dot_general x3, matrix products, attend(): jnp.einsum('hik,khd->ihd', weights, value_heads, precision=lax.Precision....  16.8 us
    unnamed x71, local copies, waits for them, and re-layouts  16.2 us
    dot_general x3, matrix products, attend(): jnp.einsum('ihd,mchd->himc', query_heads, key_heads, precision=lax.Precis...  15.2 us
    all_to_all x1, starting transfers between devices, body(): lax.all_to_all(outgoing, 'ctx', split_axis=0, concat_axis=0, tiled=True)  10.9 us
  transfers between devices with their start and end apart: 12, of which 6 were waited for; matrix products, arithmetic and copies ran while one was open for 12% of the time, Pallas kernels for 0%

profile of v1, /device:TPU:8, one launch (start us, length us, event | category | flops | bytes accessed | tf_op | source)
XLA Modules:
  0.0 457.8 jit_solution(7410197727473687348)
XLA Ops:
  7.2 2.0 copy.154
  9.2 5.5 %all-to-all-start.1 = ((f32[128,8,96]{0,2,1:T(8,128)}), f32[128,8,96]{0,2,1:T(8,128)S(1)}, u32[]{:S(2)}, u32[]{:S(2)}) async-start(f32[128,8,96]{0,2,1:T(8,128)} %bitcast.3), calls=%async_computation.1 | async-start | bytes 786432 | tf_op jit(solution)/shard_map/all_to_all | solution.py:46
  15.8 1.9 copy.153
  18.0 4.2 all-to-all-done.1
  22.2 4.8 %all-to-all-start = ((f32[128,8,96]{0,2,1:T(8,128)}), f32[128,8,96]{0,2,1:T(8,128)S(1)}, u32[]{:S(2)}, u32[]{:S(2)}) async-start(f32[128,8,96]{0,2,1:T(8,128)} %bitcast), calls=%async_computation | async-start | bytes 786432 | tf_op jit(solution)/shard_map/all_to_all | solution.py:45
  27.1 7.4 %all-to-all-done = f32[128,8,96]{0,2,1:T(8,128)S(1)} async-done(((f32[128,8,96]{0,2,1:T(8,128)}), f32[128,8,96]{0,2,1:T(8,128)S(1)}, u32[]{:S(2)}, u32[]{:S(2)}) %all-to-all-start) | async-done | bytes 393248 | tf_op jit(solution)/shard_map/all_to_all | solution.py:45
  34.5 2.4 gather_fusion
  37.0 4.0 broadcast_select_fusion.1
  41.0 10.9 %all-to-all-start.2 = ((f32[32,128,192]{1,2,0:T(8,128)}), f32[32,128,192]{1,2,0:T(8,128)}, u32[]{:S(2)}, u32[]{:S(2)}) async-start(f32[32,128,192]{1,2,0:T(8,128)} %broadcast_select_fusion.1), calls=%async_computation.2 | async-start | bytes 6291456 | tf_op jit(solution)/shard_map/all_to_all | solution.py:64
  52.2 0.9 copy.167
  53.3 72.7 %all-to-all-done.2 = f32[32,128,192]{1,2,0:T(8,128)} async-done(((f32[32,128,192]{1,2,0:T(8,128)}), f32[32,128,192]{1,2,0:T(8,128)}, u32[]{:S(2)}, u32[]{:S(2)}) %all-to-all-start.2) | async-done | bytes 3145760 | tf_op jit(solution)/shard_map/all_to_all | solution.py:64
  126.0 4.8 %all-to-all-start.3 = ((f32[128,8,96]{0,2,1:T(8,128)}), f32[128,8,96]{0,2,1:T(8,128)S(1)}, u32[]{:S(2)}, u32[]{:S(2)}) async-start(f32[128,8,96]{0,2,1:T(8,128)} %bitcast.13), calls=%async_computation.3 | async-start | bytes 786432 | tf_op jit(solution)/shard_map/all_to_all | solution.py:44
  131.5 1.6 copy.170
  134.2 2.5 gather_fusion.1
  136.7 1.6 pad_maximum_fusion.2
  138.3 4.8 %all-to-all-start.5 = ((f32[128,8,96]{0,2,1:T(8,128)}), f32[128,8,96]{0,2,1:T(8,128)S(1)}, u32[]{:S(2)}, u32[]{:S(2)}) async-start(f32[128,8,96]{0,2,1:T(8,128)} %bitcast.154), calls=%async_computation.5 | async-start | bytes 786432 | tf_op jit(solution)/shard_map/all_to_all | solution.py:47
  143.2 7.1 %fusion.19 = (f32[8,2,128]{2,1,0:T(2,128)S(1)}, f32[8,2,128,3,128]{2,4,3,1,0:T(8,128)S(1)}) fusion(f32[8,128,3,128]{1,3,2,0:T(8,128)} %bitcast.132, f32[2]{0:T(128)S(1)} %copy-done.22, f32[8,128,2,48,1]{1,3,4,2,0:T(8,128)} %bitcast.145, f32[8,3,128,2,48]{2,4,3,1,0:T(8,128)} %bitcast.134), kind=kOutput, calls=%fused_computation.74 | convolution fusion | flops 456128512 | bytes 6299656 | tf_op jit(solution)/shard_map/jvp(vmap(ihd,mchd->himc))/dot_general | solution.py:20
  151.5 2.0 copy.166
  153.5 3.4 reshape.372
  157.5 6.8 %fusion = (f32[8,2,128]{2,1,0:T(2,128)S(1)}, f32[8,2,384,128]{3,2,1,0:T(8,128)S(1)}) fusion(f32[8,2,128,3,128]{2,4,3,1,0:T(8,128)S(1)} %get-tuple-element.50, f32[8,2,128]{2,1,0:T(2,128)} %multiply_divide_fusion, f32[8,2,128]{2,1,0:T(2,128)S(1)} %get-tuple-element.49, f32[8,384,2,48]{1,3,2,0:T(8,128)} %reshape.372, f32[8,2,48,128]{3,2,1,0:T(8,128)S(1)} %bitcast.143), kind=kOutput, calls=%fused_computation.8 | convolution fusion | flops 456128512 | bytes 7888896 | tf_op jit(solution)/shard_map/transpose(jvp(vmap(hik,khd->ihd)))/dot_general | solution.py:28
  164.3 2.9 multiply_reduce_fusion
  167.6 1.3 copy-done.4
  168.8 5.0 %convolution_bitcast_fusion = f32[8,384,2,48]{1,3,2,0:T(8,128)} fusion(f32[8,2,128,384]{2,3,1,0:T(8,128)S(1)} %get-tuple-element.41, f32[8,2,48,128]{3,2,1,0:T(8,128)S(1)} %bitcast.144), kind=kOutput, calls=%fused_computation.23 | convolution fusion | flops 452984832 | bytes 4718592 | tf_op jit(solution)/shard_map/transpose(jvp(vmap(hik,khd->ihd)))/dot_general | solution.py:28
  173.8 3.0 reshape.376
  176.9 5.1 %convolution_bitcast_fusion.1 = f32[8,3,128,2,48]{2,4,1,3,0:T(8,128)S(1)} fusion(f32[8,2,128,3,128]{2,4,3,1,0:T(8,128)S(1)} %bitcast.130, f32[8,128,2,48,1]{1,3,4,2,0:T(8,128)} %bitcast.146), kind=kOutput, calls=%fused_computation.24 | convolution fusion | flops 452984832 | bytes 4718592 | tf_op jit(solution)/shard_map/transpose(jvp(vmap(ihd,mchd->himc)))/dot_general | solution.py:20
  183.1 2.0 broadcast_in_dim.27
  185.1 4.0 scatter_fusion
  189.2 5.6 %all-to-all-start.7 = ((f32[32,128,192]{1,2,0:T(8,128)}), f32[32,128,192]{1,2,0:T(8,128)}, u32[]{:S(2)}, u32[]{:S(2)}) async-start(f32[32,128,192]{1,2,0:T(8,128)} %scatter_fusion), calls=%async_computation.7 | async-start | bytes 6291456 | tf_op jit(solution)/shard_map/all_to_all | solution.py:97
  195.2 1.6 copy.185
  197.0 4.5 scatter_fusion.2
  201.5 1.0 copy-done.6
  202.5 1.0 slice_bitcast_fusion.2
  203.6 5.0 %fusion.20 = f32[8,2,48,128]{3,2,1,0:T(8,128)} fusion(f32[8,384,2,48]{1,3,2,0:T(8,128)S(1)} %copy-done.8, f32[8,2,128,384]{2,3,1,0:T(8,128)} %copy-done.4), kind=kOutput, calls=%fused_computation.75 | convolution fusion | flops 452984832 | bytes 4718592 | tf_op jit(solution)/shard_map/jvp(vmap(hik,khd->ihd))/dot_general | solution.py:28
  208.6 3.0 fusion.4
  211.6 64.7 %all-to-all-done.7 = f32[32,128,192]{1,2,0:T(8,128)} async-done(((f32[32,128,192]{1,2,0:T(8,128)}), f32[32,128,192]{1,2,0:T(8,128)}, u32[]{:S(2)}, u32[]{:S(2)}) %all-to-all-start.7) | async-done | bytes 3145760 | tf_op jit(solution)/shard_map/all_to_all | solution.py:97
  276.3 5.1 %all-to-all-start.4 = ((f32[8,128,96]{1,2,0:T(8,128)}), f32[8,128,96]{1,2,0:T(8,128)S(1)}, u32[]{:S(2)}, u32[]{:S(2)}) async-start(f32[8,128,96]{1,2,0:T(8,128)} %bitcast.23), calls=%async_computation.4 | async-start | bytes 786432 | tf_op jit(solution)/shard_map/all_to_all | solution.py:84
  281.5 4.0 broadcast_select_fusion
  285.5 5.6 %scatter_fusion.1 = f32[8,128,192]{1,2,0:T(8,128)S(1)} fusion(f32[8,128,192]{1,2,0:T(8,128)S(1)} %pad_maximum_fusion.4, s32[32]{0:T(128)S(1)} %copy-done.25, f32[32,128,192]{1,2,0:T(8,128)} %broadcast_select_fusion), kind=kCustom, calls=%fused_computation.4 | custom fusion | flops 786432 | bytes 9437312 | tf_op jit(solution)/shard_map/scatter-add | solution.py:99
  291.1 4.8 %all-to-all-start.6 = ((f32[8,128,96]{1,2,0:T(8,128)}), f32[8,128,96]{1,2,0:T(8,128)S(1)}, u32[]{:S(2)}, u32[]{:S(2)}) async-start(f32[8,128,96]{1,2,0:T(8,128)} %bitcast.36), calls=%async_computation.6 | async-start | bytes 786432 | tf_op jit(solution)/shard_map/all_to_all | solution.py:87
  296.8 6.5 %all-to-all-done.6 = f32[8,128,96]{1,2,0:T(8,128)S(1)} async-done(((f32[8,128,96]{1,2,0:T(8,128)}), f32[8,128,96]{1,2,0:T(8,128)S(1)}, u32[]{:S(2)}, u32[]{:S(2)}) %all-to-all-start.6) | async-done | bytes 393248 | tf_op jit(solution)/shard_map/all_to_all | solution.py:87
  303.3 4.8 %all-to-all-start.8 = ((f32[8,128,96]{1,2,0:T(8,128)}), f32[8,128,96]{1,2,0:T(8,128)S(1)}, u32[]{:S(2)}, u32[]{:S(2)}) async-start(f32[8,128,96]{1,2,0:T(8,128)} %bitcast.129), calls=%async_computation.8 | async-start | bytes 786432 | tf_op jit(solution)/shard_map/all_to_all | solution.py:102
  308.1 58.3 %all-reduce.3.cloned.1.call-done = f32[16,128,128]{2,1,0:T(8,128)} async-done(((f32[16,128,128]{2,1,0:T(8,128)}), f32[16,128,128]{2,1,0:T(8,128)}) %all-reduce.3.cloned.1.call-update) | async-done | bytes 1048592 | tf_op jit(solution)/shard_map/psum | solution.py:110
  367.2 4.8 %all-to-all-start.9 = ((f32[8,128,96]{1,2,0:T(8,128)}), f32[8,128,96]{1,2,0:T(8,128)S(1)}, u32[]{:S(2)}, u32[]{:S(2)}) async-start(f32[8,128,96]{1,2,0:T(8,128)} %bitcast.128), calls=%async_computation.9 | async-start | bytes 786432 | tf_op jit(solution)/shard_map/all_to_all | solution.py:103
  372.1 72.7 %psum.23 = f32[2]{0:T(128)} all-reduce(f32[2]{0:T(128)S(1)} %copy-done.28), channel_id=1, replica_groups=mesh['ctx'=32,'head'=8] {'ctx'}, use_global_device_ids=true, to_apply=%region_13.14 | all-reduce | flops 2 | bytes 16 | tf_op jit(solution)/shard_map/psum | solution.py:111
  445.7 0.9 copy.187
  446.6 0.9 copy.188
  447.5 0.9 copy.189
  448.5 2.3 copy.218
  (112 shorter events, 10.1 us)
Async XLA Ops:
  7.2 123.7 %copy-start = (f32[16,128,128]{2,1,0:T(8,128)S(1)}, f32[16,128,128]{2,1,0:T(8,128)}, u32[]{:S(2)}) copy-start(f32[16,128,128]{2,1,0:T(8,128)} %param.14) | copy-start | bytes 3145732
  9.2 13.0 %all-to-all-start.1 = ((f32[128,8,96]{0,2,1:T(8,128)}), f32[128,8,96]{0,2,1:T(8,128)S(1)}, u32[]{:S(2)}, u32[]{:S(2)}) async-start(f32[128,8,96]{0,2,1:T(8,128)} %bitcast.3), calls=%async_computation.1 | async-start | bytes 786432 | tf_op jit(solution)/shard_map/all_to_all | solution.py:46
  18.0 19.0 %copy-start.20 = (pred[32]{0:T(512)(128)(4,1)}, pred[32]{0:T(512)(128)(4,1)S(1)}, u32[]{:S(2)}) copy-start(pred[32]{0:T(512)(128)(4,1)S(1)} %get-tuple-element.39) | copy-start | bytes 100
  22.2 12.3 %all-to-all-start = ((f32[128,8,96]{0,2,1:T(8,128)}), f32[128,8,96]{0,2,1:T(8,128)S(1)}, u32[]{:S(2)}, u32[]{:S(2)}) async-start(f32[128,8,96]{0,2,1:T(8,128)} %bitcast), calls=%async_computation | async-start | bytes 786432 | tf_op jit(solution)/shard_map/all_to_all | solution.py:45
  27.0 10.0 %copy-start.24 = (s32[32]{0:T(128)}, s32[32]{0:T(128)S(1)}, u32[]{:S(2)}) copy-start(s32[32]{0:T(128)S(1)} %fusion.14) | copy-start | bytes 388
  34.5 2.5 copy-start.14
  41.0 11.0 %copy-start.18 = (s32[8,3]{0,1:T(4,128)S(1)}, s32[8,3]{0,1:T(4,128)}, u32[]{:S(2)}) copy-start(s32[8,3]{0,1:T(4,128)} %param.13) | copy-start | bytes 292
  41.0 11.1 %copy-start.16 = (f32[128,768]{1,0:T(8,128)S(1)}, f32[128,768]{1,0:T(8,128)}, u32[]{:S(2)}) copy-start(f32[128,768]{1,0:T(8,128)} %param.8) | copy-start | bytes 1179652
  41.0 85.0 %all-to-all-start.2 = ((f32[32,128,192]{1,2,0:T(8,128)}), f32[32,128,192]{1,2,0:T(8,128)}, u32[]{:S(2)}, u32[]{:S(2)}) async-start(f32[32,128,192]{1,2,0:T(8,128)} %broadcast_select_fusion.1), calls=%async_computation.2 | async-start | bytes 6291456 | tf_op jit(solution)/shard_map/all_to_all | solution.py:64
  53.3 72.8 %copy-start.26 = (s32[16]{0:T(128)}, s32[16]{0:T(128)S(1)}, u32[]{:S(2)}) copy-start(s32[16]{0:T(128)S(1)} %fusion.15) | copy-start | bytes 196
  126.0 12.3 %all-to-all-start.3 = ((f32[128,8,96]{0,2,1:T(8,128)}), f32[128,8,96]{0,2,1:T(8,128)S(1)}, u32[]{:S(2)}, u32[]{:S(2)}) async-start(f32[128,8,96]{0,2,1:T(8,128)} %bitcast.13), calls=%async_computation.3 | async-start | bytes 786432 | tf_op jit(solution)/shard_map/all_to_all | solution.py:44
  131.5 1.7 copy-start.17
  131.5 2.6 copy-start.15
  136.7 6.5 %copy-start.22 = (f32[2]{0:T(128)S(1)}, f32[2]{0:T(128)}, u32[]{:S(2)}) copy-start(f32[2]{0:T(128)} %param.15) | copy-start | bytes 28
  138.3 4.8 %copy-start.13 = (f32[128,8,96]{0,2,1:T(8,128)}, f32[128,8,96]{0,2,1:T(8,128)S(1)}, u32[]{:S(2)}) copy-start(f32[128,8,96]{0,2,1:T(8,128)S(1)} %all-to-all-done.3) | copy-start | bytes 1179652
  138.3 19.1 %all-to-all-start.5 = ((f32[128,8,96]{0,2,1:T(8,128)}), f32[128,8,96]{0,2,1:T(8,128)S(1)}, u32[]{:S(2)}, u32[]{:S(2)}) async-start(f32[128,8,96]{0,2,1:T(8,128)} %bitcast.154), calls=%async_computation.5 | async-start | bytes 786432 | tf_op jit(solution)/shard_map/all_to_all | solution.py:47
  150.2 1.3 copy-start.12
  157.5 6.9 %copy-start.5 = (f32[8,3,128,128]{2,3,1,0:T(8,128)S(1)}, f32[8,3,128,128]{2,3,1,0:T(8,128)}, u32[]{:S(2)}) copy-start(f32[8,3,128,128]{2,3,1,0:T(8,128)} %copy.170) | copy-start | bytes 4718596
  157.5 6.9 %copy-start.23 = (f32[2]{0:T(128)S(1)}, f32[2]{0:T(128)}, u32[]{:S(2)}) copy-start(f32[2]{0:T(128)} %param.15) | copy-start | bytes 28
  167.2 1.6 copy-start.4
  167.5 9.3 %copy-start.2 = (f32[8,2,128,384]{2,3,1,0:T(8,128)}, f32[8,2,128,384]{2,3,1,0:T(8,128)S(1)}, u32[]{:S(2)}) copy-start(f32[8,2,128,384]{2,3,1,0:T(8,128)S(1)} %broadcast_multiply_fusion) | copy-start | bytes 9437188
  176.8 5.2 %copy-start.10 = (f32[8,3,128,96]{2,1,3,0:T(4,128)S(1)}, f32[8,3,128,96]{2,1,3,0:T(4,128)}, u32[]{:S(2)}) copy-start(f32[8,3,128,96]{2,1,3,0:T(4,128)} %reshape.376) | copy-start | bytes 3538948
  182.1 1.0 copy-start.11
  182.6 2.5 copy-start.27
  189.2 5.6 %copy-start.19 = (s32[8,3]{0,1:T(4,128)S(1)}, s32[8,3]{0,1:T(4,128)}, u32[]{:S(2)}) copy-start(s32[8,3]{0,1:T(4,128)} %param.13) | copy-start | bytes 292
  189.2 5.8 %copy-start.9 = (f32[8,128,384]{1,2,0:T(8,128)S(1)}, f32[8,128,384]{1,2,0:T(8,128)}, u32[]{:S(2)}) copy-start(f32[8,128,384]{1,2,0:T(8,128)} %get-tuple-element.37) | copy-start | bytes 4718596
  189.2 87.2 %all-to-all-start.7 = ((f32[32,128,192]{1,2,0:T(8,128)}), f32[32,128,192]{1,2,0:T(8,128)}, u32[]{:S(2)}, u32[]{:S(2)}) async-start(f32[32,128,192]{1,2,0:T(8,128)} %scatter_fusion), calls=%async_computation.7 | async-start | bytes 6291456 | tf_op jit(solution)/shard_map/all_to_all | solution.py:97
  194.7 171.7 %all-reduce.3.cloned.1.call-start = ((), (), s32[]{:S(2)}) async-start(), calls=%async_computation.10 | async-start | bytes 2097152 | tf_op jit(solution)/shard_map/psum | solution.py:110
  197.0 6.5 %slice-start = ((f32[8,3,128,96]{2,1,3,0:T(4,128)}), f32[8,1,128,96]{2,1,3,0:T(1,128)S(1)}, s32[]{:S(2)}) async-start(f32[8,3,128,96]{2,1,3,0:T(4,128)} %reshape.376), calls=%async_computation.12 | async-start | bytes 786432 | tf_op jit(solution)/shard_map/slice | solution.py:98
  197.0 6.6 %copy-start.8 = (f32[8,384,2,48]{1,3,2,0:T(8,128)S(1)}, f32[8,384,2,48]{1,3,2,0:T(8,128)}, u32[]{:S(2)}) copy-start(f32[8,384,2,48]{1,3,2,0:T(8,128)} %reshape.372) | copy-start | bytes 3538948
  201.5 1.0 copy-start.6
  203.5 5.1 %copy-start.3 = (f32[8,2,128,384]{2,3,1,0:T(8,128)S(1)}, f32[8,2,128,384]{2,3,1,0:T(8,128)}, u32[]{:S(2)}) copy-start(f32[8,2,128,384]{2,3,1,0:T(8,128)} %copy-done.2) | copy-start | bytes 9437188
  203.5 5.1 %copy-start.7 = (f32[8,3,128,96]{2,3,1,0:T(8,128)S(1)}, f32[8,3,128,96]{2,3,1,0:T(8,128)}, u32[]{:S(2)}) copy-start(f32[8,3,128,96]{2,3,1,0:T(8,128)} %get-tuple-element.42) | copy-start | bytes 3538948
  208.6 72.8 %copy-start.21 = (pred[32]{0:T(512)(128)(4,1)S(1)}, pred[32]{0:T(512)(128)(4,1)}, u32[]{:S(2)}) copy-start(pred[32]{0:T(512)(128)(4,1)} %copy-done.20) | copy-start | bytes 100
  276.3 14.7 %all-to-all-start.4 = ((f32[8,128,96]{1,2,0:T(8,128)}), f32[8,128,96]{1,2,0:T(8,128)S(1)}, u32[]{:S(2)}, u32[]{:S(2)}) async-start(f32[8,128,96]{1,2,0:T(8,128)} %bitcast.23), calls=%async_computation.4 | async-start | bytes 786432 | tf_op jit(solution)/shard_map/all_to_all | solution.py:84
  281.5 4.0 copy-start.25
  291.1 12.3 %all-to-all-start.6 = ((f32[8,128,96]{1,2,0:T(8,128)}), f32[8,128,96]{1,2,0:T(8,128)S(1)}, u32[]{:S(2)}, u32[]{:S(2)}) async-start(f32[8,128,96]{1,2,0:T(8,128)} %bitcast.36), calls=%async_computation.6 | async-start | bytes 786432 | tf_op jit(solution)/shard_map/all_to_all | solution.py:87
  296.0 76.1 %copy-start.28 = (f32[2]{0:T(128)S(1)}, f32[2]{0:T(128)}, u32[]{:S(2)}) copy-start(f32[2]{0:T(128)} %get-tuple-element.36) | copy-start | bytes 28
  303.3 63.9 %all-to-all-start.8 = ((f32[8,128,96]{1,2,0:T(8,128)}), f32[8,128,96]{1,2,0:T(8,128)S(1)}, u32[]{:S(2)}, u32[]{:S(2)}) async-start(f32[8,128,96]{1,2,0:T(8,128)} %bitcast.129), calls=%async_computation.8 | async-start | bytes 786432 | tf_op jit(solution)/shard_map/all_to_all | solution.py:102
  308.1 140.3 %all-reduce.5.cloned.1.call-start = ((), (), s32[]{:S(2)}) async-start(), calls=%async_computation.11 | async-start | bytes 2097152 | tf_op jit(solution)/shard_map/psum | solution.py:110
  366.4 84.3 %copy-start.1 = (f32[16,128,128]{2,1,0:T(8,128)S(1)}, f32[16,128,128]{2,1,0:T(8,128)}, u32[]{:S(2)}) copy-start(f32[16,128,128]{2,1,0:T(8,128)} %param.14) | copy-start | bytes 3145732
  367.2 80.3 %all-to-all-start.9 = ((f32[8,128,96]{1,2,0:T(8,128)}), f32[8,128,96]{1,2,0:T(8,128)S(1)}, u32[]{:S(2)}, u32[]{:S(2)}) async-start(f32[8,128,96]{1,2,0:T(8,128)} %bitcast.128), calls=%async_computation.9 | async-start | bytes 786432 | tf_op jit(solution)/shard_map/all_to_all | solution.py:103
Sparse Core Ops, SparseCore 0:
  202.6 163.7 all-reduce.2
  368.8 63.1 all-reduce.4
